TPU v7x, 32 devices: a whole 2x2x4 slice. The times are simulated.
32 devices in a mesh: tile: 8 (over z, core), grp: 4 (over y, x).
Axes of the slice: x: 2, y: 2, z: 4, core: 2. Of those that a mesh axis runs over, the one named last changes fastest.
Arguments:
- spectra: bfloat16 [128, 16, 1024], P(('tile', 'grp')), may hold values from -320 to 320
- validity: int32 [128, 16], P(('tile', 'grp')), may hold values 0 or 1
- source_lists: int32 [8, 4, 16], P(None, 'grp'), may hold values from 0 to 127, as said below
Outputs:
- correlations: bfloat16 [8, 4, 16, 16, 2048], P('tile', 'grp')
Inputs may be any that keep to these rules, and one draw needn't show every extreme that they name: `source_lists`: entry [t, g, j] names a channel held by a device of grp index g, that is (entry // 4) % 4 == g; the 16 entries of one list are distinct; at most 2 entries of one list are held by any one device, and in every list some device holds exactly 2.
All inputs are finite; a program needn't handle non-finite values. No bound on the sum of `validity` on one device may be relied on, other than what follows from the above.
Results may differ from a plain program's by a relative error of at most 0.0066.
Values may be sent and summed in bfloat16 or wider, within the bound.
No kernel may reach another device: no remote copies, remote signals or barrier semaphores. Data moves between devices by JAX's collectives and lax.ppermute only.
A program may use at most 128 MiB of HBM per device.

v0:
```python
import math
import jax
import jax.numpy as jnp
from jax import lax
from jax.sharding import PartitionSpec as P

LAGS = 2048
SMOOTH = 64
EPSILON = 1e-06


def box_mean(magnitude, reach):
    bin_count = magnitude.shape[-1]
    lead_shape = magnitude.shape[:-1]
    running = jnp.cumsum(magnitude, axis=-1)
    prefix = jnp.concatenate([jnp.zeros(lead_shape + (1,), magnitude.dtype), running], axis=-1)
    tail = jnp.broadcast_to(prefix[..., -1:], lead_shape + (reach,))
    upper = jnp.concatenate([prefix[..., reach + 1 :], tail], axis=-1)
    lower = jnp.concatenate(
        [jnp.zeros(lead_shape + (reach,), magnitude.dtype), prefix[..., : bin_count - reach]],
        axis=-1,
    )
    bin_index = jnp.arange(bin_count, dtype=jnp.int32)
    counted = jnp.minimum(bin_index + reach + 1, bin_count) - jnp.maximum(bin_index - reach, 0)
    return (upper - lower) / counted.astype(magnitude.dtype)


def whiten(spectra, reach):
    bin_count = spectra.shape[-1] // 2
    real_part = spectra[..., :bin_count].astype(jnp.float32)
    imag_part = spectra[..., bin_count:].astype(jnp.float32)
    magnitude = jnp.sqrt(real_part * real_part + imag_part * imag_part)
    smoothed = box_mean(magnitude, reach)
    inverse = 1.0 / (smoothed + EPSILON)
    return jnp.concatenate([real_part * inverse, imag_part * inverse], axis=-1).astype(jnp.bfloat16)


def lag_table(bin_count, lag_count):
    frequency = jnp.arange(bin_count, dtype=jnp.int32)[:, None]
    lag_shift = jnp.arange(lag_count, dtype=jnp.int32)[None, :] - lag_count // 2
    phase_index = frequency * lag_shift % (2 * lag_count)
    angles = phase_index.astype(jnp.float32) * (math.pi / lag_count)
    return jnp.concatenate([jnp.cos(angles), -jnp.sin(angles)], axis=0).astype(jnp.bfloat16)


def correlate(source_rows, source_mask, panel_rows, panel_mask, lag_basis):
    bin_count = source_rows.shape[-1] // 2
    masked_source = source_rows * source_mask[:, :, None]
    masked_panel = panel_rows * panel_mask[:, :, None]
    source_real = masked_source[..., :bin_count]
    source_imag = masked_source[..., bin_count:]
    panel_real = masked_panel[..., :bin_count]
    panel_imag = masked_panel[..., bin_count:]
    real_sum = jnp.einsum(
        "swf,rwf->srf", source_real, panel_real, preferred_element_type=jnp.float32
    ) + jnp.einsum("swf,rwf->srf", source_imag, panel_imag, preferred_element_type=jnp.float32)
    imag_sum = jnp.einsum(
        "swf,rwf->srf", source_real, panel_imag, preferred_element_type=jnp.float32
    ) - jnp.einsum("swf,rwf->srf", source_imag, panel_real, preferred_element_type=jnp.float32)
    shared_count = jnp.dot(source_mask, panel_mask.T, preferred_element_type=jnp.float32)
    weight = (1.0 / jnp.maximum(shared_count, 1.0))[:, :, None]
    stacked = jnp.concatenate([real_sum * weight, imag_sum * weight], axis=-1).astype(jnp.bfloat16)
    lagged = jnp.dot(
        stacked.reshape(-1, 2 * bin_count), lag_basis, preferred_element_type=jnp.float32
    )
    lagged = lagged * (1.0 / math.sqrt(bin_count))
    return lagged.reshape(source_rows.shape[0], panel_rows.shape[0], -1).astype(jnp.bfloat16)


def body(spectra, validity, source_lists):
    group_count = lax.axis_size("grp")
    ch_local = spectra.shape[0]
    row_width = spectra.shape[2]
    tile_here = lax.axis_index("tile")
    all_lists = source_lists[:, 0, :]
    block_span = ch_local * group_count
    own_list = lax.dynamic_index_in_dim(all_lists, tile_here, 0, keepdims=False)
    owner_tile = own_list // block_span
    local_row = own_list % ch_local
    mask_rows = validity.astype(jnp.bfloat16)
    ready = whiten(spectra, SMOOTH)
    column_rows, column_mask = (
        lax.all_gather(ready, "tile", axis=0, tiled=True),
        lax.all_gather(mask_rows, "tile", axis=0, tiled=True),
    )
    picked = owner_tile * ch_local + local_row
    source_rows = jnp.take(column_rows, picked, axis=0)
    source_mask = jnp.take(column_mask, picked, axis=0)
    panel_rows, panel_mask = (
        lax.all_gather(ready, "grp", axis=0, tiled=True),
        lax.all_gather(mask_rows, "grp", axis=0, tiled=True),
    )
    lag_basis = lag_table(row_width // 2, LAGS)
    lagged = correlate(source_rows, source_mask, panel_rows, panel_mask, lag_basis)
    return lagged[None, None]


def solution(mesh):
    in_specs = (P(("tile", "grp"), None, None), P(("tile", "grp"), None), P(None, "grp", None))
    out_specs = P("tile", "grp", None, None, None)
    return jax.shard_map(body, mesh=mesh, in_specs=in_specs, out_specs=out_specs, check_vma=False)
```

profile of v0, /device:TPU:0, one launch (start us, length us, event | category | flops | bytes accessed | tf_op | source)
XLA Modules:
  0.0 140.3 jit_solution(8925865290935990632)
XLA Ops:
  6.5 0.0 all-gather.4.cloned.1.call-start
  6.5 0.9 copy_bitcast_fusion.1
  7.5 4.6 %reduce-window.6 = f32[4,16,4,128]{3,1,2,0:T(8,128)S(1)} reduce-window(f32[4,16,4,128]{3,1,2,0:T(8,128)S(1)} %copy_bitcast_fusion.1, f32[]{:T(128)} %constant.90.clone.1), window={size=1x1x1x128 pad=0_0x0_0x0_0x127_0}, to_apply=%region_0.1 | reduce-window | flops 4161536 | bytes 262148 | tf_op jit(solution)/shard_map/reduce-window
  12.0 0.2 slice_reduce_fusion
  12.3 0.1 copy_bitcast_fusion
  12.4 0.1 fusion.52
  12.5 0.2 slice_reduce_fusion.1
  12.7 0.1 broadcast_in_dim.37
  12.8 1.0 fusion.37
  13.7 0.9 fusion.38
  14.6 0.7 pad_maximum_fusion
  15.3 0.0 all-gather.4.cloned.1.call-update
  15.3 0.7 fusion.48
  16.0 0.7 compare_and_fusion
  16.6 11.9 %all_gather.12 = bf16[16,16,1024]{2,1,0:T(8,128)(2,1)S(1)} all-gather(bf16[4,16,1024]{2,1,0:T(8,128)(2,1)} %pad_maximum_fusion), channel_id=1, replica_groups=mesh['tile'=8,'grp'=4] {'grp'}, dimensions={0}, use_global_device_ids=true | all-gather | bytes 655360 | tf_op jit(solution)/shard_map/all_gather | solution.py:90
  28.5 0.7 convert_bitcast_fusion
  29.2 12.0 %all-gather.1 = bf16[8,4,16]{2,1,0:T(4,128)(2,1)S(1)} all-gather(bf16[1,4,16]{2,1,0:T(4,128)(2,1)S(1)} %convert_bitcast_fusion), channel_id=1, replica_groups=mesh['tile'=8,'grp'=4] {'tile'}, dimensions={0}, use_global_device_ids=true | all-gather | bytes 1152 | tf_op jit(solution)/shard_map/all_gather | solution.py:84
  41.2 7.7 %all-gather = bf16[4,4,16]{2,1,0:T(4,128)(2,1)S(1)} all-gather(bf16[1,4,16]{2,1,0:T(4,128)(2,1)S(1)} %convert_bitcast_fusion), channel_id=1, replica_groups=mesh['tile'=8,'grp'=4] {'grp'}, dimensions={0}, use_global_device_ids=true | all-gather | bytes 640 | tf_op jit(solution)/shard_map/all_gather | solution.py:91
  48.9 4.7 %copy.39 = bf16[16,16,1024]{1,0,2:T(8,128)(2,1)} copy(bf16[16,16,1024]{2,1,0:T(8,128)(2,1)S(1)} %all_gather.12) | data formatting | bytes 1048576 | tf_op jit(solution)/shard_map/all_gather | solution.py:90
  53.6 0.0 copy-start
  53.6 4.5 %fusion.66 = bf16[16,16,1024]{1,0,2:T(8,128)(2,1)} fusion(bf16[16,16,1024]{1,0,2:T(8,128)(2,1)} %copy.39, bf16[16,16]{1,0:T(8,128)(2,1)S(1)} %bitcast.68), kind=kLoop, calls=%fused_computation.18.clone.1 | loop fusion | flops 262144 | bytes 1049088 | tf_op jit(solution)/shard_map/swf,rwf->srf/dot_general | solution.py:56
  58.2 0.0 copy-done
  58.2 2.2 %fusion.70 = bf16[16,16,1024]{1,0,2:T(8,128)(2,1)} fusion(bf16[16,16,1024]{1,0,2:T(8,128)(2,1)S(1)} %copy-done, bf16[16,16]{1,0:T(8,128)(2,1)S(1)} %bitcast.69), kind=kLoop, calls=%fused_computation.22.clone | loop fusion | flops 262144 | bytes 1049088 | tf_op jit(solution)/shard_map/swf,rwf->srf/dot_general | solution.py:57
  60.4 0.6 gather_fusion.1
  61.0 0.1 broadcast_select_fusion
  61.1 0.7 fusion.28
  61.8 4.6 %fusion.72 = bf16[16,16,1024]{1,0,2:T(8,128)(2,1)} fusion(bf16[16,16,1024]{1,0,2:T(8,128)(2,1)} %copy.39, bf16[16,16]{1,0:T(8,128)(2,1)S(1)} %bitcast.71), kind=kLoop, calls=%fused_computation.24.clone | loop fusion | flops 262144 | bytes 1049088 | tf_op jit(solution)/shard_map/swf,rwf->srf/dot_general | solution.py:59
  66.4 0.0 copy-done.1
  66.4 2.2 %fusion.68 = bf16[16,16,1024]{1,0,2:T(8,128)(2,1)} fusion(bf16[16,16,1024]{1,0,2:T(8,128)(2,1)S(1)} %copy-done.1, bf16[16,16]{1,0:T(8,128)(2,1)S(1)} %bitcast.72), kind=kLoop, calls=%fused_computation.20.clone.1 | loop fusion | flops 262144 | bytes 1049088 | tf_op jit(solution)/shard_map/swf,rwf->srf/dot_general | solution.py:54
  68.6 18.0 %cosine_convert_fusion = (bf16[512,2048]{1,0:T(8,128)(2,1)}, bf16[512,2048]{1,0:T(8,128)(2,1)}) fusion(s32[2048]{0:T(1024)S(1)} %iota_add_fusion), kind=kLoop, calls=%fused_computation.13 | loop fusion | flops 17825792 | bytes 4202496 | tf_op jit(solution)/shard_map/convert
  86.7 0.0 all-gather.4.cloned.1.call-done
  86.7 1.8 %gather_fusion = bf16[16,16,1024]{2,1,0:T(8,128)(2,1)S(1)} fusion(bf16[32,16,1024]{2,1,0:T(8,128)(2,1)} %all-gather.4.cloned.1.call-done, s32[1024]{0:T(1024)S(1)} %pad_clamp_fusion), kind=kCustom, calls=%fused_computation | custom fusion | bytes 1048640 | tf_op jit(solution)/shard_map/jit(_take)/gather | solution.py:87
  88.5 0.1 select_multiply_fusion
  88.6 0.8 fusion.51
  89.4 2.0 %copy.41 = bf16[16,16,512]{1,0,2:T(8,128)(2,1)S(1)} copy(bf16[16,16,512]{2,1,0:T(8,128)(2,1)S(1)} %get-tuple-element.7) | data formatting | bytes 524288 | tf_op jit(solution)/shard_map/slice | solution.py:51
  91.3 0.0 copy-start.2
  91.3 5.5 %fusion.10 = f32[512,16,16]{2,1,0:T(8,128)} fusion(bf16[16,16,512]{1,0,2:T(8,128)(2,1)S(1)} %copy.41, bf16[16,16,1024]{1,0,2:T(8,128)(2,1)} %fusion.66), kind=kOutput, calls=%fused_computation.17 | convolution fusion | flops 4194304 | bytes 1310720 | tf_op jit(solution)/shard_map/swf,rwf->srf/dot_general | solution.py:56
  96.8 0.0 copy-done.2
  96.8 0.0 copy-start.9
  96.8 3.6 %copy.43 = f32[512,16,16]{0,1,2:T(8,128)} copy(f32[512,16,16]{2,1,0:T(8,128)} %fusion.10) | data formatting | bytes 1048576 | tf_op jit(solution)/shard_map/swf,rwf->srf/dot_general | solution.py:56
  100.5 0.0 copy-done.9
  100.5 2.0 %copy.40 = bf16[16,16,512]{1,0,2:T(8,128)(2,1)S(1)} copy(bf16[16,16,512]{2,1,0:T(8,128)(2,1)S(1)} %copy-done.9) | data formatting | bytes 524288 | tf_op jit(solution)/shard_map/slice | solution.py:50
  102.5 0.0 copy-start.4
  102.5 1.3 copy-done.4
  103.8 4.7 %fusion.14 = f32[512,16,16]{2,1,0:T(8,128)} fusion(bf16[16,16,512]{1,0,2:T(8,128)(2,1)S(1)} %copy.40, bf16[16,16,1024]{1,0,2:T(8,128)(2,1)} %fusion.70), kind=kOutput, calls=%fused_computation.21 | convolution fusion | flops 4194304 | bytes 1310720 | tf_op jit(solution)/shard_map/swf,rwf->srf/dot_general | solution.py:57
  108.5 0.0 copy-start.3
  108.5 3.8 %copy.46 = f32[512,16,16]{0,1,2:T(8,128)} copy(f32[512,16,16]{2,1,0:T(8,128)} %fusion.14) | data formatting | bytes 1048576 | tf_op jit(solution)/shard_map/swf,rwf->srf/dot_general | solution.py:57
  112.3 0.0 copy-done.3
  112.3 4.8 %fusion.16 = f32[512,16,16]{2,1,0:T(8,128)} fusion(bf16[16,16,512]{1,0,2:T(8,128)(2,1)S(1)} %copy-done.3, bf16[16,16,1024]{1,0,2:T(8,128)(2,1)} %fusion.72), kind=kOutput, calls=%fused_computation.23 | convolution fusion | flops 4194304 | bytes 1310720 | tf_op jit(solution)/shard_map/swf,rwf->srf/dot_general | solution.py:59
  117.0 0.0 copy-start.5
  117.1 3.8 %copy.47 = f32[512,16,16]{0,1,2:T(8,128)} copy(f32[512,16,16]{2,1,0:T(8,128)} %fusion.16) | data formatting | bytes 1048576 | tf_op jit(solution)/shard_map/swf,rwf->srf/dot_general | solution.py:59
  120.8 0.0 copy-done.5
  120.9 4.8 %fusion.12 = f32[512,16,16]{2,1,0:T(8,128)} fusion(bf16[16,16,512]{1,0,2:T(8,128)(2,1)S(1)} %copy-done.5, bf16[16,16,1024]{1,0,2:T(8,128)(2,1)} %fusion.68), kind=kOutput, calls=%fused_computation.19 | convolution fusion | flops 4194304 | bytes 1310720 | tf_op jit(solution)/shard_map/swf,rwf->srf/dot_general | solution.py:54
  125.6 0.0 copy-start.6
  125.6 0.0 copy-start.7
  125.6 0.0 copy-start.8
  125.6 0.0 copy-start.10
  125.6 3.1 %copy.42 = f32[512,16,16]{0,1,2:T(8,128)S(1)} copy(f32[512,16,16]{2,1,0:T(8,128)} %fusion.12) | data formatting | bytes 1048576 | tf_op jit(solution)/shard_map/swf,rwf->srf/dot_general | solution.py:54
  128.7 0.0 copy-done.6
  128.7 0.0 copy-done.7
  128.8 0.0 copy-done.8
  128.8 0.0 copy-done.10
  128.8 0.2 fusion.33
  129.0 4.5 %fusion.21 = bf16[256,2048]{1,0:T(8,128)(2,1)} fusion(bf16[512,2048]{1,0:T(8,128)(2,1)} %get-tuple-element.14, bf16[512,2048]{1,0:T(8,128)(2,1)} %get-tuple-element.13, bf16[256,512]{1,0:T(8,128)(2,1)S(1)} %bitcast.66, bf16[256,512]{1,0:T(8,128)(2,1)S(1)} %bitcast.65), kind=kOutput, calls=%fused_computation.26 | convolution fusion | flops 1084227584 | bytes 5767168 | tf_op jit(solution)/shard_map/dot_general | solution.py:63
  (6 shorter events, 0.1 us)
Async XLA Ops:
  6.5 80.1 %all-gather.4.cloned.1.call-start = ((), (), s32[]{:S(2)}) async-start(), calls=%async_computation | async-start | bytes 1179648 | tf_op jit(solution)/shard_map/all_gather | solution.py:83
  53.6 4.6 %copy-start = (bf16[16,16,1024]{1,0,2:T(8,128)(2,1)S(1)}, bf16[16,16,1024]{1,0,2:T(8,128)(2,1)}, u32[]{:S(2)}) copy-start(bf16[16,16,1024]{1,0,2:T(8,128)(2,1)} %copy.39) | copy-start | bytes 1572868
  61.8 4.6 %copy-start.1 = (bf16[16,16,1024]{1,0,2:T(8,128)(2,1)S(1)}, bf16[16,16,1024]{1,0,2:T(8,128)(2,1)}, u32[]{:S(2)}) copy-start(bf16[16,16,1024]{1,0,2:T(8,128)(2,1)} %copy.39) | copy-start | bytes 1572868
  91.3 5.5 %copy-start.2 = (bf16[16,16,512]{1,0,2:T(8,128)(2,1)}, bf16[16,16,512]{1,0,2:T(8,128)(2,1)S(1)}, u32[]{:S(2)}) copy-start(bf16[16,16,512]{1,0,2:T(8,128)(2,1)S(1)} %copy.41) | copy-start | bytes 786436
  96.8 3.6 %copy-start.9 = (bf16[16,16,512]{2,1,0:T(8,128)(2,1)S(1)}, bf16[16,16,512]{2,1,0:T(8,128)(2,1)}, u32[]{:S(2)}) copy-start(bf16[16,16,512]{2,1,0:T(8,128)(2,1)} %get-tuple-element.8) | copy-start | bytes 786436
  102.5 1.3 copy-start.4
  108.5 3.8 %copy-start.3 = (bf16[16,16,512]{1,0,2:T(8,128)(2,1)S(1)}, bf16[16,16,512]{1,0,2:T(8,128)(2,1)}, u32[]{:S(2)}) copy-start(bf16[16,16,512]{1,0,2:T(8,128)(2,1)} %copy-done.2) | copy-start | bytes 786436
  117.0 3.8 %copy-start.5 = (bf16[16,16,512]{1,0,2:T(8,128)(2,1)S(1)}, bf16[16,16,512]{1,0,2:T(8,128)(2,1)}, u32[]{:S(2)}) copy-start(bf16[16,16,512]{1,0,2:T(8,128)(2,1)} %copy-done.4) | copy-start | bytes 786436
  125.6 3.1 %copy-start.6 = (f32[512,16,16]{0,1,2:T(8,128)S(1)}, f32[512,16,16]{0,1,2:T(8,128)}, u32[]{:S(2)}) copy-start(f32[512,16,16]{0,1,2:T(8,128)} %copy.43) | copy-start | bytes 1572868
  125.6 3.1 %copy-start.7 = (f32[512,16,16]{0,1,2:T(8,128)S(1)}, f32[512,16,16]{0,1,2:T(8,128)}, u32[]{:S(2)}) copy-start(f32[512,16,16]{0,1,2:T(8,128)} %copy.46) | copy-start | bytes 1572868
  125.6 3.1 %copy-start.8 = (f32[512,16,16]{0,1,2:T(8,128)S(1)}, f32[512,16,16]{0,1,2:T(8,128)}, u32[]{:S(2)}) copy-start(f32[512,16,16]{0,1,2:T(8,128)} %copy.47) | copy-start | bytes 1572868
  125.6 3.1 %copy-start.10 = (f32[16,16]{1,0:T(8,128)S(1)}, f32[16,16]{1,0:T(8,128)}, u32[]{:S(2)}) copy-start(f32[16,16]{1,0:T(8,128)} %fusion.28) | copy-start | bytes 3076
Sparse Core Ops, SparseCore 0:
  15.4 24.9 all-gather.3
where the time goes:
time: 141 us; the launch traced here: 140 us
  other arithmetic  42.2 us (30%)
  blocking collectives  31.6 us (22%)
  local copies, waits for them, and re-layouts  28 us (20%)
  matrix products  25 us (18%)
  between operations  13.6 us (10%)
    another operation x7, other arithmetic  24.7 us
    all_gather x1, blocking collectives, body(): lax.all_gather(mask_rows, 'tile', axis=0, tiled=True)  12 us
    all_gather x1, blocking collectives, body(): lax.all_gather(ready, 'grp', axis=0, tiled=True)  11.9 us
    all_gather x1, blocking collectives, body(): lax.all_gather(mask_rows, 'grp', axis=0, tiled=True)  7.7 us
    dot_general x1, matrix products, correlate(): jnp.einsum('swf,rwf->srf', source_imag, panel_imag, preferred_element_typ...  5.49 us
    dot_general x1, matrix products, correlate(): jnp.einsum('swf,rwf->srf', source_real, panel_real, preferred_element_typ...  4.78 us
    dot_general x1, matrix products, correlate(): jnp.einsum('swf,rwf->srf', source_imag, panel_real, preferred_element_typ...  4.76 us
    dot_general x1, matrix products, correlate(): jnp.einsum('swf,rwf->srf', source_real, panel_imag, preferred_element_typ...  4.73 us
  transfers between devices with their start and end apart: 1, of which 0 were waited for; matrix products, arithmetic and copies ran while one was open for 28% of the time, Pallas kernels for 0%

commit v1 on v0

--- a/solution.py
+++ b/solution.py
@@ -7,6 +7,25 @@
 LAGS = 2048
 SMOOTH = 64
 EPSILON = 1e-06
+
+
+def ring_gather(array, axis, dim):
+    size, mine, rows = (lax.axis_size(axis), lax.axis_index(axis), array.shape[dim])
+    upward = [(i, (i + 1) % size) for i in range(size)]
+    left = [(i, (i - 1) % size) for i in range(size)]
+    out = jnp.zeros((*array.shape[:dim], size * rows, *array.shape[dim + 1 :]), array.dtype)
+    out = lax.dynamic_update_slice_in_dim(out, array, mine * rows, axis=dim)
+    from_left = from_right = array
+    middle = size // 2
+    for step in range(1, middle + 1):
+        from_left = lax.ppermute(from_left, axis, upward)
+        out = lax.dynamic_update_slice_in_dim(out, from_left, (mine - step) % size * rows, axis=dim)
+        if step < size - middle:
+            from_right = lax.ppermute(from_right, axis, left)
+            out = lax.dynamic_update_slice_in_dim(
+                out, from_right, (mine + step) % size * rows, axis=dim
+            )
+    return out
 
 
 def box_mean(magnitude, reach):
@@ -87,7 +106,7 @@
     source_rows = jnp.take(column_rows, picked, axis=0)
     source_mask = jnp.take(column_mask, picked, axis=0)
     panel_rows, panel_mask = (
-        lax.all_gather(ready, "grp", axis=0, tiled=True),
+        ring_gather(ready, "grp", 0),
         lax.all_gather(mask_rows, "grp", axis=0, tiled=True),
     )
     lag_basis = lag_table(row_width // 2, LAGS)

time: 141 us -> 148 us (1.050)
  blocking collectives: 31.6 us -> 20.5 us
  local copies, waits for them, and re-layouts: 28 us -> 35 us
  starting transfers between devices: 0.01 us -> 4.72 us
  other arithmetic: 42.2 us -> 45.7 us
  waiting for transfers between devices: 0.02 us -> 2.5 us
    all_gather x1 -> x0, blocking collectives: 11.9 us -> none  [body(): lax.all_gather(ready, 'grp', axis=0, tiled=True)]
    dynamic_update_slice x0 -> x4, local copies, waits for them, and re-layouts: none -> 5.63 us  [the longest x2 2.87 us: ring_gather(): lax.dynamic_update_slice_in_dim(out, from_left, (mine - step) % size * ro...]
    all_gather x1 -> x0, local copies, waits for them, and re-layouts: 4.72 us -> none  [body(): lax.all_gather(ready, 'grp', axis=0, tiled=True)]
    ppermute x0 -> x3, starting transfers between devices: none -> 4.72 us  [the longest x2 3.69 us: ring_gather(): from_left = lax.ppermute(from_left, axis, upward)]
    broadcast_in_dim x0 -> x1, local copies, waits for them, and re-layouts: none -> 2.48 us  [ring_gather(): jnp.zeros((*array.shape[:dim], size * rows, *array.shape[dim + 1:]), arra...]
    ppermute x0 -> x3, waiting for transfers between devices: none -> 2.48 us  [the longest x2 2.48 us: ring_gather(): from_left = lax.ppermute(from_left, axis, upward)]
    dot_general x1, other arithmetic: 2.24 us -> 4.43 us  [correlate(): jnp.einsum('swf,rwf->srf', source_real, panel_imag, preferred_element_typ...]
    dot_general x1, other arithmetic: 2.21 us -> 4.41 us  [correlate(): jnp.einsum('swf,rwf->srf', source_real, panel_real, preferred_element_typ...]
  transfers between devices with their start and end apart: 1 -> 4, of which waited for: 0 -> 1; matrix products, arithmetic and copies ran while one was open for 28% -> 35% of each run, Pallas kernels for 0% -> 0%
where the time goes in v1:
time: 148 us; the launch traced here: 147 us
  other arithmetic  45.7 us (31%)
  local copies, waits for them, and re-layouts  35 us (24%)
  matrix products  25 us (17%)
  blocking collectives  20.5 us (14%)
  between operations  13.7 us (9%)
  starting transfers between devices  4.72 us (3%)
  waiting for transfers between devices  2.5 us (2%)
    another operation x7, other arithmetic  24.8 us
    all_gather x1, blocking collectives, body(): lax.all_gather(mask_rows, 'tile', axis=0, tiled=True)  12 us
    all_gather x1, blocking collectives, body(): lax.all_gather(mask_rows, 'grp', axis=0, tiled=True)  8.49 us
    dot_general x1, matrix products, correlate(): jnp.einsum('swf,rwf->srf', source_imag, panel_imag, preferred_element_typ...  5.49 us
    dot_general x1, matrix products, correlate(): jnp.einsum('swf,rwf->srf', source_real, panel_real, preferred_element_typ...  4.77 us
    dot_general x1, matrix products, correlate(): jnp.einsum('swf,rwf->srf', source_imag, panel_real, preferred_element_typ...  4.76 us
    dot_general x1, matrix products, correlate(): jnp.einsum('swf,rwf->srf', source_real, panel_imag, preferred_element_typ...  4.72 us
    dot_general x1, matrix products, correlate(): jnp.dot(stacked.reshape(-1, 2 * bin_count), lag_basis, preferred_element_...  4.55 us
  transfers between devices with their start and end apart: 4, of which 1 were waited for; matrix products, arithmetic and copies ran while one was open for 35% of the time, Pallas kernels for 0%

profile of v1, /device:TPU:0, one launch (start us, length us, event | category | flops | bytes accessed | tf_op | source)
XLA Modules:
  0.0 147.1 jit_solution(15462794712300790785)
XLA Ops:
  6.5 0.0 all-gather.4.cloned.1.call-start
  6.5 0.9 copy_bitcast_fusion.1
  7.5 4.6 %reduce-window.6 = f32[4,16,4,128]{3,1,2,0:T(8,128)S(1)} reduce-window(f32[4,16,4,128]{3,1,2,0:T(8,128)S(1)} %copy_bitcast_fusion.1, f32[]{:T(128)} %constant.113.clone.1), window={size=1x1x1x128 pad=0_0x0_0x0_0x127_0}, to_apply=%region_0.1 | reduce-window | flops 4161536 | bytes 262148 | tf_op jit(solution)/shard_map/reduce-window
  12.0 0.2 slice_reduce_fusion
  12.3 0.1 copy_bitcast_fusion
  12.4 0.1 fusion.52
  12.5 0.2 slice_reduce_fusion.1
  12.7 0.1 broadcast_in_dim.41
  12.8 1.0 fusion.37
  13.7 0.9 fusion.38
  14.6 0.0 copy-start.7
  14.6 3.0 %collective-permute-start = (bf16[4,16,1024]{2,1,0:T(8,128)(2,1)S(1)}, bf16[4,16,1024]{2,1,0:T(8,128)(2,1)S(1)}, u32[]{:S(2)}, u32[]{:S(2)}) collective-permute-start(bf16[4,16,1024]{2,1,0:T(8,128)(2,1)S(1)} %pad_maximum_fusion), channel_id=1, source_target_pairs={{0,1},{1,2},{2,3},{3,0},{4,5},{5,6},{6,7},{7,4},{8,9},{9,10},{10,1... | collective-permute-start | bytes 393224 | tf_op jit(solution)/shard_map/ppermute | solution.py:21
  17.7 1.0 collective-permute-start.1
  18.7 0.0 copy-done.7
  18.7 0.0 all-gather.4.cloned.1.call-update
  18.7 1.5 %copy.45 = bf16[4,16,1024]{1,0,2:T(4,128)(2,1)S(1)} copy(bf16[4,16,1024]{2,1,0:T(8,128)(2,1)} %copy-done.7) | data formatting | bytes 262144 | tf_op jit(solution)/shard_map/concatenate | solution.py:54
  20.3 0.7 convert_bitcast_fusion
  21.0 8.5 %all-gather = bf16[4,4,16]{2,1,0:T(4,128)(2,1)S(1)} all-gather(bf16[1,4,16]{2,1,0:T(4,128)(2,1)S(1)} %convert_bitcast_fusion), channel_id=1, replica_groups=mesh['tile'=8,'grp'=4] {'grp'}, dimensions={0}, use_global_device_ids=true | all-gather | bytes 640 | tf_op jit(solution)/shard_map/all_gather | solution.py:110
  29.5 12.0 %all-gather.1 = bf16[8,4,16]{2,1,0:T(4,128)(2,1)S(1)} all-gather(bf16[1,4,16]{2,1,0:T(4,128)(2,1)S(1)} %convert_bitcast_fusion), channel_id=1, replica_groups=mesh['tile'=8,'grp'=4] {'tile'}, dimensions={0}, use_global_device_ids=true | all-gather | bytes 1152 | tf_op jit(solution)/shard_map/all_gather | solution.py:103
  41.5 0.7 fusion.48
  42.1 0.7 compare_and_fusion
  42.8 18.2 %cosine_convert_fusion = (bf16[512,2048]{1,0:T(8,128)(2,1)}, bf16[512,2048]{1,0:T(8,128)(2,1)}) fusion(s32[2048]{0:T(1024)S(1)} %iota_add_fusion), kind=kLoop, calls=%fused_computation.13 | loop fusion | flops 17825792 | bytes 4202496 | tf_op jit(solution)/shard_map/convert
  61.0 0.6 gather_fusion.1
  61.6 0.1 broadcast_select_fusion
  61.6 0.7 fusion.28
  62.4 2.5 %broadcast_in_dim.39 = bf16[16,16,1024]{1,0,2:T(8,128)(2,1)} broadcast(bf16[]{:T(256)} %constant.111.clone.1), dimensions={} | broadcast | bytes 524290 | tf_op jit(solution)/shard_map/broadcast_in_dim | solution.py:16
  64.9 1.4 constant_dynamic-update-slice_fusion.3
  66.2 0.0 collective-permute-done
  66.2 0.7 copy.46
  66.9 0.7 collective-permute-start.2
  67.6 1.5 constant_dynamic-update-slice_fusion.2
  69.0 0.0 collective-permute-done.1
  69.0 0.7 copy.47
  69.7 1.4 constant_dynamic-update-slice_fusion.1
  71.1 2.5 %collective-permute-done.2 = bf16[4,16,1024]{2,1,0:T(8,128)(2,1)S(1)} collective-permute-done((bf16[4,16,1024]{2,1,0:T(8,128)(2,1)S(1)}, bf16[4,16,1024]{2,1,0:T(8,128)(2,1)S(1)}, u32[]{:S(2)}, u32[]{:S(2)}) %collective-permute-start.2) | collective-permute-done | bytes 131104 | tf_op jit(solution)/shard_map/ppermute | solution.py:21
  73.6 0.7 copy.48
  74.3 1.4 constant_dynamic-update-slice_fusion
  75.7 4.4 %fusion.66 = bf16[16,16,1024]{1,0,2:T(8,128)(2,1)} fusion(bf16[16,16,1024]{1,0,2:T(8,128)(2,1)} %constant_dynamic-update-slice_fusion, bf16[16,16]{1,0:T(8,128)(2,1)S(1)} %bitcast.69), kind=kLoop, calls=%fused_computation.18.clone.1 | loop fusion | flops 262144 | bytes 1049088 | tf_op jit(solution)/shard_map/swf,rwf->srf/dot_general | solution.py:75
  80.1 4.4 %fusion.70 = bf16[16,16,1024]{1,0,2:T(8,128)(2,1)} fusion(bf16[16,16,1024]{1,0,2:T(8,128)(2,1)} %constant_dynamic-update-slice_fusion, bf16[16,16]{1,0:T(8,128)(2,1)S(1)} %bitcast.70), kind=kLoop, calls=%fused_computation.22.clone | loop fusion | flops 262144 | bytes 1049088 | tf_op jit(solution)/shard_map/swf,rwf->srf/dot_general | solution.py:76
  84.5 4.4 %fusion.72 = bf16[16,16,1024]{1,0,2:T(8,128)(2,1)} fusion(bf16[16,16,1024]{1,0,2:T(8,128)(2,1)} %constant_dynamic-update-slice_fusion, bf16[16,16]{1,0:T(8,128)(2,1)S(1)} %bitcast.71), kind=kLoop, calls=%fused_computation.24.clone | loop fusion | flops 262144 | bytes 1049088 | tf_op jit(solution)/shard_map/swf,rwf->srf/dot_general | solution.py:78
  89.0 4.4 %fusion.68 = bf16[16,16,1024]{1,0,2:T(8,128)(2,1)} fusion(bf16[16,16,1024]{1,0,2:T(8,128)(2,1)} %constant_dynamic-update-slice_fusion, bf16[16,16]{1,0:T(8,128)(2,1)S(1)} %bitcast.72), kind=kLoop, calls=%fused_computation.20.clone.1 | loop fusion | flops 262144 | bytes 1049088 | tf_op jit(solution)/shard_map/swf,rwf->srf/dot_general | solution.py:73
  93.4 1.8 %gather_fusion = bf16[16,16,1024]{2,1,0:T(8,128)(2,1)S(1)} fusion(bf16[32,16,1024]{2,1,0:T(8,128)(2,1)} %all-gather.4.cloned.1.call-done, s32[1024]{0:T(1024)S(1)} %pad_clamp_fusion), kind=kCustom, calls=%fused_computation | custom fusion | bytes 1048640 | tf_op jit(solution)/shard_map/jit(_take)/gather | solution.py:106
  95.2 0.1 select_multiply_fusion
  95.3 0.8 fusion.51
  96.1 2.0 %copy.50 = bf16[16,16,512]{1,0,2:T(8,128)(2,1)S(1)} copy(bf16[16,16,512]{2,1,0:T(8,128)(2,1)S(1)} %get-tuple-element.7) | data formatting | bytes 524288 | tf_op jit(solution)/shard_map/slice | solution.py:70
  98.1 0.0 copy-start
  98.1 5.5 %fusion.10 = f32[512,16,16]{2,1,0:T(8,128)} fusion(bf16[16,16,512]{1,0,2:T(8,128)(2,1)S(1)} %copy.50, bf16[16,16,1024]{1,0,2:T(8,128)(2,1)} %fusion.66), kind=kOutput, calls=%fused_computation.17 | convolution fusion | flops 4194304 | bytes 1310720 | tf_op jit(solution)/shard_map/swf,rwf->srf/dot_general | solution.py:75
  103.6 0.0 copy-done
  103.6 3.6 %copy.52 = f32[512,16,16]{0,1,2:T(8,128)} copy(f32[512,16,16]{2,1,0:T(8,128)} %fusion.10) | data formatting | bytes 1048576 | tf_op jit(solution)/shard_map/swf,rwf->srf/dot_general | solution.py:75
  107.2 0.0 copy-done.8
  107.2 2.0 %copy.49 = bf16[16,16,512]{1,0,2:T(8,128)(2,1)S(1)} copy(bf16[16,16,512]{2,1,0:T(8,128)(2,1)S(1)} %copy-done.8) | data formatting | bytes 524288 | tf_op jit(solution)/shard_map/slice | solution.py:69
  109.2 0.0 copy-start.2
  109.2 1.3 copy-done.2
  110.5 4.7 %fusion.14 = f32[512,16,16]{2,1,0:T(8,128)} fusion(bf16[16,16,512]{1,0,2:T(8,128)(2,1)S(1)} %copy.49, bf16[16,16,1024]{1,0,2:T(8,128)(2,1)} %fusion.70), kind=kOutput, calls=%fused_computation.21 | convolution fusion | flops 4194304 | bytes 1310720 | tf_op jit(solution)/shard_map/swf,rwf->srf/dot_general | solution.py:76
  115.2 3.8 %copy.55 = f32[512,16,16]{0,1,2:T(8,128)} copy(f32[512,16,16]{2,1,0:T(8,128)} %fusion.14) | data formatting | bytes 1048576 | tf_op jit(solution)/shard_map/swf,rwf->srf/dot_general | solution.py:76
  119.0 0.0 copy-done.1
  119.0 4.8 %fusion.16 = f32[512,16,16]{2,1,0:T(8,128)} fusion(bf16[16,16,512]{1,0,2:T(8,128)(2,1)S(1)} %copy-done.1, bf16[16,16,1024]{1,0,2:T(8,128)(2,1)} %fusion.72), kind=kOutput, calls=%fused_computation.23 | convolution fusion | flops 4194304 | bytes 1310720 | tf_op jit(solution)/shard_map/swf,rwf->srf/dot_general | solution.py:78
  123.8 3.8 %copy.56 = f32[512,16,16]{0,1,2:T(8,128)} copy(f32[512,16,16]{2,1,0:T(8,128)} %fusion.16) | data formatting | bytes 1048576 | tf_op jit(solution)/shard_map/swf,rwf->srf/dot_general | solution.py:78
  127.6 0.0 copy-done.3
  127.6 4.8 %fusion.12 = f32[512,16,16]{2,1,0:T(8,128)} fusion(bf16[16,16,512]{1,0,2:T(8,128)(2,1)S(1)} %copy-done.3, bf16[16,16,1024]{1,0,2:T(8,128)(2,1)} %fusion.68), kind=kOutput, calls=%fused_computation.19 | convolution fusion | flops 4194304 | bytes 1310720 | tf_op jit(solution)/shard_map/swf,rwf->srf/dot_general | solution.py:73
  132.4 3.1 %copy.51 = f32[512,16,16]{0,1,2:T(8,128)S(1)} copy(f32[512,16,16]{2,1,0:T(8,128)} %fusion.12) | data formatting | bytes 1048576 | tf_op jit(solution)/shard_map/swf,rwf->srf/dot_general | solution.py:73
  135.5 0.0 copy-done.4
  135.5 0.2 fusion.33
  135.7 4.5 %fusion.21 = bf16[256,2048]{1,0:T(8,128)(2,1)} fusion(bf16[512,2048]{1,0:T(8,128)(2,1)} %get-tuple-element.14, bf16[512,2048]{1,0:T(8,128)(2,1)} %get-tuple-element.13, bf16[256,512]{1,0:T(8,128)(2,1)S(1)} %bitcast.66, bf16[256,512]{1,0:T(8,128)(2,1)S(1)} %bitcast.65), kind=kOutput, calls=%fused_computation.26 | convolution fusion | flops 1084227584 | bytes 5767168 | tf_op jit(solution)/shard_map/dot_general | solution.py:82
  (17 shorter events, 0.1 us)
Async XLA Ops:
  6.5 86.8 %all-gather.4.cloned.1.call-start = ((), (), s32[]{:S(2)}) async-start(), calls=%async_computation | async-start | bytes 1179648 | tf_op jit(solution)/shard_map/all_gather | solution.py:102
  14.6 4.1 %copy-start.7 = (bf16[4,16,1024]{2,1,0:T(8,128)(2,1)}, bf16[4,16,1024]{2,1,0:T(8,128)(2,1)S(1)}, u32[]{:S(2)}) copy-start(bf16[4,16,1024]{2,1,0:T(8,128)(2,1)S(1)} %pad_maximum_fusion) | copy-start | bytes 393220
  14.6 51.6 %collective-permute-start = (bf16[4,16,1024]{2,1,0:T(8,128)(2,1)S(1)}, bf16[4,16,1024]{2,1,0:T(8,128)(2,1)S(1)}, u32[]{:S(2)}, u32[]{:S(2)}) collective-permute-start(bf16[4,16,1024]{2,1,0:T(8,128)(2,1)S(1)} %pad_maximum_fusion), channel_id=1, source_target_pairs={{0,1},{1,2},{2,3},{3,0},{4,5},{5,6},{6,7},{7,4},{8,9},{9,10},{10,1... | collective-permute-start | bytes 393224 | tf_op jit(solution)/shard_map/ppermute | solution.py:21
  17.7 51.4 %collective-permute-start.1 = (bf16[4,16,1024]{2,1,0:T(8,128)(2,1)S(1)}, bf16[4,16,1024]{2,1,0:T(8,128)(2,1)S(1)}, u32[]{:S(2)}, u32[]{:S(2)}) collective-permute-start(bf16[4,16,1024]{2,1,0:T(8,128)(2,1)S(1)} %pad_maximum_fusion), channel_id=1, source_target_pairs={{0,3},{1,0},{2,1},{3,2},{4,7},{5,4},{6,5},{7,6},{8,11},{9,8},{10,9... | collective-permute-start | bytes 393224 | tf_op jit(solution)/shard_map/ppermute | solution.py:24
  66.9 6.7 %collective-permute-start.2 = (bf16[4,16,1024]{2,1,0:T(8,128)(2,1)S(1)}, bf16[4,16,1024]{2,1,0:T(8,128)(2,1)S(1)}, u32[]{:S(2)}, u32[]{:S(2)}) collective-permute-start(bf16[4,16,1024]{2,1,0:T(8,128)(2,1)S(1)} %collective-permute-done), channel_id=1, source_target_pairs={{0,1},{1,2},{2,3},{3,0},{4,5},{5,6},{6,7},{7,4},{8,9},{9,10},{10,1... | collective-permute-start | bytes 393224 | tf_op jit(solution)/shard_map/ppermute | solution.py:21
  98.1 5.5 %copy-start = (bf16[16,16,512]{1,0,2:T(8,128)(2,1)}, bf16[16,16,512]{1,0,2:T(8,128)(2,1)S(1)}, u32[]{:S(2)}) copy-start(bf16[16,16,512]{1,0,2:T(8,128)(2,1)S(1)} %copy.50) | copy-start | bytes 786436
  103.6 3.6 %copy-start.8 = (bf16[16,16,512]{2,1,0:T(8,128)(2,1)S(1)}, bf16[16,16,512]{2,1,0:T(8,128)(2,1)}, u32[]{:S(2)}) copy-start(bf16[16,16,512]{2,1,0:T(8,128)(2,1)} %get-tuple-element.8) | copy-start | bytes 786436
  109.2 1.3 copy-start.2
  115.2 3.8 %copy-start.1 = (bf16[16,16,512]{1,0,2:T(8,128)(2,1)S(1)}, bf16[16,16,512]{1,0,2:T(8,128)(2,1)}, u32[]{:S(2)}) copy-start(bf16[16,16,512]{1,0,2:T(8,128)(2,1)} %copy-done) | copy-start | bytes 786436
  123.8 3.8 %copy-start.3 = (bf16[16,16,512]{1,0,2:T(8,128)(2,1)S(1)}, bf16[16,16,512]{1,0,2:T(8,128)(2,1)}, u32[]{:S(2)}) copy-start(bf16[16,16,512]{1,0,2:T(8,128)(2,1)} %copy-done.2) | copy-start | bytes 786436
  132.3 3.1 %copy-start.4 = (f32[512,16,16]{0,1,2:T(8,128)S(1)}, f32[512,16,16]{0,1,2:T(8,128)}, u32[]{:S(2)}) copy-start(f32[512,16,16]{0,1,2:T(8,128)} %copy.52) | copy-start | bytes 1572868
  132.4 3.1 %copy-start.5 = (f32[512,16,16]{0,1,2:T(8,128)S(1)}, f32[512,16,16]{0,1,2:T(8,128)}, u32[]{:S(2)}) copy-start(f32[512,16,16]{0,1,2:T(8,128)} %copy.55) | copy-start | bytes 1572868
  132.4 3.1 %copy-start.6 = (f32[512,16,16]{0,1,2:T(8,128)S(1)}, f32[512,16,16]{0,1,2:T(8,128)}, u32[]{:S(2)}) copy-start(f32[512,16,16]{0,1,2:T(8,128)} %copy.56) | copy-start | bytes 1572868
  132.4 3.1 %copy-start.9 = (f32[16,16]{1,0:T(8,128)S(1)}, f32[16,16]{1,0:T(8,128)}, u32[]{:S(2)}) copy-start(f32[16,16]{1,0:T(8,128)} %fusion.28) | copy-start | bytes 3076
Sparse Core Ops, SparseCore 0:
  18.8 22.9 all-gather.3
